TPU v7x, 32 devices: a whole 2x2x4 slice. The times are simulated.
32 devices in a mesh: dp: 8 (over z, x), seq: 4 (over y, core).
Axes of the slice: x: 2, y: 2, z: 4, core: 2. Of those that a mesh axis runs over, the one named last changes fastest.
Arguments:
- tokens: bfloat16 [8, 1024, 768], P('dp', 'seq'), may hold values from -6 to 6
- segment_ids: int32 [8, 1024], P('dp'), may hold values from 0 to 5, never falling along the last dimension, each value on 1 to 512 neighbouring positions
- pad_lengths: int32 [8], P('dp'), may hold values from 0 to 511
- threshold: float32 [1], replicated, may hold values from 0.05 to 2
- gains: float32 [2, 768], replicated, may hold values from 0.5 to 1.5
- gain_first: float32 [2, 768], replicated, may hold values from -256 to 256
- gain_second: float32 [2, 768], replicated, may hold values from 2048 to 8192
- slot_tiles: int32 [448], replicated, may hold values from 0 to 447, as said below
- weight_slots: float32 [448, 128, 128], P(('dp', 'seq')), may hold values from -2 to 2
- first_moment: float32 [448, 128, 128], P(('dp', 'seq')), may hold values from -160 to 160
- second_moment: float32 [448, 128, 128], P(('dp', 'seq')), may hold values from 819.2 to 3276.8
- basis_left: float32 [448, 128, 128], P(('dp', 'seq')), may hold values from -1 to 1, as said below
- basis_right: float32 [448, 128, 128], P(('dp', 'seq')), may hold values from -1 to 1, as said below
- out_grad: bfloat16 [8, 1024, 768], P('dp', 'seq'), may hold values from -6 to 6
Outputs:
- output: bfloat16 [8, 1024, 768], P('dp', 'seq')
- input_grad: float32 [8, 1024, 768], P('dp', 'seq')
- fraction: float32 [8], P('dp')
- moment_first: float32 [448, 128, 128], P(('dp', 'seq'))
- moment_second: float32 [448, 128, 128], P(('dp', 'seq'))
- new_weights: float32 [448, 128, 128], P(('dp', 'seq'))
- gain_update: float32 [2, 768], replicated
- gain_moment: float32 [2, 768], replicated
- gain_square: float32 [2, 768], replicated
Inputs may be any that keep to these rules, and one draw needn't show every extreme that they name: `segment_ids`: segment numbers never fall along a row; each segment has 1 to 512 positions, one exactly that many. `slot_tiles`: a permutation of the slot numbers; a slot whose entry is 432 or more holds no tile. `basis_left`: each slot's matrix is orthogonal. `basis_right`: each slot's matrix is orthogonal.
All inputs are finite; a program needn't handle non-finite values.
Results may differ from a plain program's by a relative error of at most 0.011.
Values may be sent and summed in bfloat16 or wider, within the bound.
No kernel may reach another device: no remote copies, remote signals or barrier semaphores. Data moves between devices by JAX's collectives and lax.ppermute only.
A program may use at most 192 MiB of HBM per device.

v0:
```python
import jax
import jax.numpy as jnp
from jax import lax
from jax.sharding import PartitionSpec as P

H = 12
HD = 64
FF = 3072
STEP = 3
select_scale = 0.2
fraction_slope = 2.0
first_decay = 0.5
second_decay = 0.5
adam_epsilon = 1e-08
weight_rate = 0.05
gain_rate = 0.2
decay_rate = 0.1
norm_epsilon = 1e-05
precise = lax.Precision.HIGHEST


def carried_in(value, axis, join, neutral, backward):
    count, mine = (lax.axis_size(axis), lax.axis_index(axis))
    pieces = lax.all_gather(value, axis)
    if backward:
        pieces = pieces[::-1]
        mine = count - 1 - mine
    total = jnp.full_like(value, 0) + jnp.asarray(neutral, value.dtype)

    def step(position, total):
        longer = join(total, pieces[position])
        return jnp.where(position < mine, longer, total)

    return lax.fori_loop(0, count - 1, step, total)


def layer_norm(values, gain):
    centred = values - jnp.mean(values, axis=-1, keepdims=True)
    spread = jnp.mean(centred * centred, axis=-1, keepdims=True)
    return centred * lax.rsqrt(spread + norm_epsilon) * gain


def gelu_local(values):
    return jax.nn.gelu(values, approximate=True)


def tiles_of(matrix, tile_side):
    height, across = matrix.shape
    shaped = matrix.reshape(height // tile_side, tile_side, across // tile_side, tile_side)
    return shaped.transpose(0, 2, 1, 3).reshape(-1, tile_side, tile_side)


def matrix_of(tile_stack, height, across):
    tile_side = tile_stack.shape[-1]
    shaped = tile_stack.reshape(height // tile_side, across // tile_side, tile_side, tile_side)
    return shaped.transpose(0, 2, 1, 3).reshape(height, across)


def split_tiles(tile_stack, width, hidden_width):
    tile_side = tile_stack.shape[-1]
    shapes = [(width, 3 * width), (width, width), (width, hidden_width), (hidden_width, width)]
    result = []
    offset = 0
    for height, across in shapes:
        count_here = height * across // (tile_side * tile_side)
        result.append(matrix_of(tile_stack[offset : offset + count_here], height, across))
        offset = offset + count_here
    return result


def slot_buffer(grads, slot_tiles, tile_side, tile_count):
    stacked = jnp.concatenate(
        [tiles_of(grad, tile_side) for grad in grads]
        + [jnp.zeros((1, tile_side, tile_side), jnp.float32)],
        axis=0,
    )
    return stacked[jnp.minimum(slot_tiles, tile_count)]


def add_single(earlier, later):
    return earlier + later


def rotated_adam(grad_slots, first, second, left, right, weight, correction):
    turned = jnp.einsum("sji,sjk->sik", left, grad_slots, precision=precise)
    turned = jnp.einsum("sik,skl->sil", turned, right, precision=precise)
    first_new = first_decay * first + (1.0 - first_decay) * turned
    second_new = second_decay * second + (1.0 - second_decay) * turned * turned
    norm_step = first_new / correction / (jnp.sqrt(second_new / correction) + adam_epsilon)
    back = jnp.einsum("sik,skl->sil", left, norm_step, precision=precise)
    back = jnp.einsum("sil,sjl->sij", back, right, precision=precise)
    return (first_new, second_new, weight - weight_rate * back - weight_rate * decay_rate * weight)


def local(
    tokens,
    segment_ids,
    pad_lengths,
    threshold,
    gains,
    gain_first,
    gain_second,
    slot_tiles,
    weight_slots,
    first_moment,
    second_moment,
    basis_left,
    basis_right,
    out_grad,
):
    rows_here, tok_local, width = tokens.shape
    length = segment_ids.shape[1]
    hidden_width = FF
    heads = H
    head_dim = HD
    tile_side = weight_slots.shape[-1]
    slot_total = slot_tiles.shape[0]
    tile_count = (4 * width * width + 2 * width * hidden_width) // (tile_side * tile_side)
    query_start = lax.axis_index("seq") * tok_local
    query_pos = query_start + jnp.arange(tok_local, dtype=jnp.int32)
    key_pos = jnp.arange(length, dtype=jnp.int32)
    shared = lax.all_gather(weight_slots.astype(jnp.bfloat16), ("dp", "seq"), axis=0, tiled=True)
    tile_ids = jnp.arange(tile_count, dtype=jnp.int32)
    slot_ids = jnp.arange(slot_total, dtype=jnp.int32)
    position = jnp.sum(
        jnp.where(slot_tiles[None, :] == tile_ids[:, None], slot_ids[None, :], 0), axis=1
    )
    w_qkv, w_out, w_up, w_down = split_tiles(shared[position], width, hidden_width)
    local_ids = jnp.arange(tok_local, dtype=jnp.int32)
    lower_ones = (local_ids[None, :] < local_ids[:, None]).astype(jnp.float32)
    empty_columns = jnp.zeros((length,), jnp.float32)
    grad_sums = (
        jnp.zeros(w_qkv.shape, jnp.float32),
        jnp.zeros(w_out.shape, jnp.float32),
        jnp.zeros(w_up.shape, jnp.float32),
        jnp.zeros(w_down.shape, jnp.float32),
    )
    seg_row = segment_ids[0]
    valid_len = length - pad_lengths[0]
    seg_query = lax.dynamic_slice_in_dim(seg_row, query_start, tok_local)
    valid_keys = key_pos < valid_len
    row_input = tokens[0].astype(jnp.float32)
    normed_pre_f, pull_pre = jax.vjp(layer_norm, row_input, gains[0])
    normed_pre = normed_pre_f.astype(jnp.bfloat16)
    projected = jnp.dot(normed_pre, w_qkv, preferred_element_type=jnp.float32)
    query_heads = projected[:, :width].astype(jnp.bfloat16).reshape(tok_local, heads, head_dim)
    key_local = projected[:, width : 2 * width].astype(jnp.bfloat16)
    value_local = projected[:, 2 * width :].astype(jnp.bfloat16)
    key_all = lax.all_gather(key_local, "seq", axis=0, tiled=True)
    value_all = lax.all_gather(value_local, "seq", axis=0, tiled=True)
    key_heads = key_all.reshape(length, heads, head_dim)
    value_heads = value_all.reshape(length, heads, head_dim)
    value_float = value_heads.astype(jnp.float32)
    allowed = (seg_query[:, None] == seg_row[None, :]) & (key_pos[None, :] <= query_pos[:, None])
    allowed = allowed & (valid_keys[None, :] | (key_pos[None, :] == query_pos[:, None]))
    strict = allowed & (key_pos[None, :] < query_pos[:, None])
    strict_float = strict.astype(jnp.float32)
    allowed_float = allowed.astype(jnp.float32)
    scores = (
        jnp.einsum("qhd,khd->hqk", query_heads, key_heads, preferred_element_type=jnp.float32)
        * 0.125
    )
    select = select_scale * jax.nn.relu(scores[0]) * strict_float
    column_part = jnp.sum(select, axis=0)
    prefix = carried_in(column_part, "seq", add_single, empty_columns, False)
    shadow = prefix[None, :] + jnp.dot(lower_ones, select, precision=precise)
    logits = jnp.where(allowed[None], scores - shadow[None], -1e30)
    row_max = jnp.max(logits, axis=2)
    exps = jnp.exp(logits - row_max[:, :, None]) * allowed_float[None]
    totals = jnp.sum(exps, axis=2)
    probs = exps / totals[:, :, None]
    mixed_out = jnp.einsum("hqk,khd->qhd", probs, value_float, precision=precise).reshape(
        tok_local, width
    )
    column_total = lax.psum(column_part, "seq")
    counted = jnp.sum(
        valid_keys.astype(jnp.float32)
        * jax.nn.sigmoid((column_total - threshold[0]) * fraction_slope)
    )
    fraction_rows = [counted / valid_len.astype(jnp.float32)]
    mixed_b = mixed_out.astype(jnp.bfloat16)
    hidden_one = row_input + jnp.dot(mixed_b, w_out, preferred_element_type=jnp.float32)
    normed_mid_f, pull_mid = jax.vjp(layer_norm, hidden_one, gains[1])
    normed_mid = normed_mid_f.astype(jnp.bfloat16)
    upper = jnp.dot(normed_mid, w_up, preferred_element_type=jnp.float32)
    active_f, pull_gelu = jax.vjp(gelu_local, upper)
    active = active_f.astype(jnp.bfloat16)
    result = hidden_one + jnp.dot(active, w_down, preferred_element_type=jnp.float32)
    output_rows = [result.astype(jnp.bfloat16)]
    row_grad = out_grad[0]
    grad_down = jnp.einsum("tf,td->fd", active, row_grad, preferred_element_type=jnp.float32)
    grad_active = jnp.einsum("td,fd->tf", row_grad, w_down, preferred_element_type=jnp.float32)
    grad_upper = pull_gelu(grad_active)[0].astype(jnp.bfloat16)
    grad_up = jnp.einsum("td,tf->df", normed_mid, grad_upper, preferred_element_type=jnp.float32)
    grad_mid = jnp.einsum("tf,df->td", grad_upper, w_up, preferred_element_type=jnp.float32)
    grad_hidden_ln, grad_gain_mid = pull_mid(grad_mid)
    grad_hidden = row_grad.astype(jnp.float32) + grad_hidden_ln
    grad_branch = grad_hidden.astype(jnp.bfloat16)
    grad_out = jnp.einsum("td,te->de", mixed_b, grad_branch, preferred_element_type=jnp.float32)
    grad_mixed = jnp.einsum(
        "te,de->td", grad_branch, w_out, preferred_element_type=jnp.float32
    ).astype(jnp.bfloat16)
    delta_rows = jnp.sum(
        (grad_mixed.astype(jnp.float32) * mixed_out).reshape(tok_local, heads, head_dim), axis=2
    )
    grad_heads = grad_mixed.reshape(tok_local, heads, head_dim)
    dprob = jnp.einsum("qhd,khd->hqk", grad_heads, value_heads, preferred_element_type=jnp.float32)
    grad_values_part = jnp.einsum(
        "hqk,qhd->khd", probs, grad_heads.astype(jnp.float32), precision=precise
    )
    dlogit = probs * (dprob - delta_rows.T[:, :, None])
    grad_shadow = -jnp.sum(dlogit, axis=0)
    shadow_columns = jnp.sum(grad_shadow, axis=0)
    suffix = carried_in(shadow_columns, "seq", add_single, empty_columns, True)
    grad_select = jnp.dot(lower_ones.T, grad_shadow, precision=precise) + suffix[None, :]
    head_zero = (
        dlogit[0]
        + grad_select * select_scale * (scores[0] > 0.0).astype(jnp.float32) * strict_float
    )
    grad_scores = jnp.concatenate([head_zero[None], dlogit[1:]], axis=0).astype(jnp.bfloat16)
    grad_query = (
        jnp.einsum("hqk,khd->qhd", grad_scores, key_heads, preferred_element_type=jnp.float32)
        * 0.125
    ).reshape(tok_local, width)
    grad_keys_part = (
        jnp.einsum("hqk,qhd->khd", grad_scores, query_heads, preferred_element_type=jnp.float32)
        * 0.125
    )
    grad_keys = lax.psum_scatter(
        grad_keys_part.reshape(length, width).astype(jnp.bfloat16),
        "seq",
        scatter_dimension=0,
        tiled=True,
    )
    grad_values = lax.psum_scatter(
        grad_values_part.reshape(length, width).astype(jnp.bfloat16),
        "seq",
        scatter_dimension=0,
        tiled=True,
    )
    grad_qkv = jnp.concatenate([grad_query.astype(jnp.bfloat16), grad_keys, grad_values], axis=1)
    grad_qkv_w = jnp.einsum("td,te->de", normed_pre, grad_qkv, preferred_element_type=jnp.float32)
    grad_pre = jnp.einsum("te,de->td", grad_qkv, w_qkv, preferred_element_type=jnp.float32)
    grad_input_ln, grad_gain_pre = pull_pre(grad_pre)
    input_rows = [grad_hidden + grad_input_ln]
    gain_grad = jnp.stack([grad_gain_pre, grad_gain_mid])
    grad_sums = (grad_qkv_w, grad_out, grad_up, grad_down)
    owned_grad = lax.psum_scatter(
        slot_buffer(grad_sums, slot_tiles, tile_side, tile_count),
        ("dp", "seq"),
        scatter_dimension=0,
        tiled=True,
    )
    gain_total = lax.psum(gain_grad, ("dp", "seq"))
    correction = 1.0 - first_decay**STEP
    moment_first, moment_second, new_weights = rotated_adam(
        owned_grad, first_moment, second_moment, basis_left, basis_right, weight_slots, correction
    )
    gain_moment = first_decay * gain_first + (1.0 - first_decay) * gain_total
    gain_square = second_decay * gain_second + (1.0 - second_decay) * gain_total * gain_total
    gain_update = gains - gain_rate * (gain_moment / correction) / (
        jnp.sqrt(gain_square / correction) + adam_epsilon
    )
    return (
        jnp.stack(output_rows),
        jnp.stack(input_rows),
        jnp.stack(fraction_rows),
        moment_first,
        moment_second,
        new_weights,
        gain_update,
        gain_moment,
        gain_square,
    )


def solution(mesh):
    in_specs = (
        P("dp", "seq", None),
        P("dp", None),
        P("dp"),
        P(),
        P(),
        P(),
        P(),
        P(),
        P(("dp", "seq"), None, None),
        P(("dp", "seq"), None, None),
        P(("dp", "seq"), None, None),
        P(("dp", "seq"), None, None),
        P(("dp", "seq"), None, None),
        P("dp", "seq", None),
    )
    out_specs = (
        P("dp", "seq", None),
        P("dp", "seq", None),
        P("dp"),
        P(("dp", "seq"), None, None),
        P(("dp", "seq"), None, None),
        P(("dp", "seq"), None, None),
        P(),
        P(),
        P(),
    )
    return jax.shard_map(local, mesh=mesh, in_specs=in_specs, out_specs=out_specs, check_vma=False)
```

profile of v0, /device:TPU:1, one launch (start us, length us, event | category | flops | bytes accessed | tf_op | source)
XLA Modules:
  0.0 714.0 jit_solution(11046674508676594106)
XLA Ops:
  7.2 2.1 convert_element_type.104
  11.1 1.1 convert_reduce_fusion
  12.2 1.2 fusion.92
  14.0 105.3 %all-gather.6.cloned.1.call-done = bf16[448,128,128]{2,1,0:T(8,128)(2,1)} async-done(((bf16[14,128,128]{2,1,0:T(8,128)(2,1)}), bf16[448,128,128]{2,1,0:T(8,128)(2,1)}) %all-gather.6.cloned.1.call-update) | async-done | bytes 14680080 | tf_op jit(solution)/shard_map/all_gather | solution.py:122
  119.3 18.3 %gather_fusion = bf16[432,128,128]{2,1,0:T(8,128)(2,1)} fusion(bf16[448,128,128]{2,1,0:T(8,128)(2,1)} %all-gather.6.cloned.1.call-done, s32[1024]{0:T(1024)S(1)} %pad_clamp_fusion.1), kind=kCustom, calls=%fused_computation | custom fusion | bytes 28313280 | tf_op jit(solution)/shard_map/gather | solution.py:128
  137.6 2.0 slice-done
  139.6 2.4 copy.73
  142.1 1.2 convolution_convert_fusion
  144.2 1.0 fusion.133
  146.4 1.5 fusion.71
  148.1 2.0 copy.77
  150.1 12.0 %fusion.132 = (bf16[144,128,128]{2,1,0:T(8,128)(2,1)}, bf16[144,128,128]{2,1,0:T(8,128)(2,1)}) fusion(bf16[432,128,128]{2,1,0:T(8,128)(2,1)} %gather_fusion), kind=kLoop, calls=%fused_computation.197 | loop fusion | bytes 18874368 | tf_op jit(solution)/shard_map/slice | solution.py:66
  162.1 6.9 copy.79
  169.0 7.5 %copy.78 = bf16[6,24,128,128]{3,1,2,0:T(8,128)(2,1)} copy(bf16[6,24,128,128]{3,2,1,0:T(8,128)(2,1)} %bitcast.240) | data formatting | bytes 9437184 | tf_op jit(solution)/shard_map/reshape | solution.py:55
  176.6 1.7 copy.76
  178.4 1.8 broadcast_multiply_fusion
  180.3 4.7 copy-done.1
  186.2 5.5 all-gather
  192.0 2.6 convolution_add_fusion.1
  194.6 17.9 %fusion.134 = (f32[12,256]{1,0:T(8,128)S(1)}, f32[12,256,1024]{2,1,0:T(8,128)}) fusion(f32[256,1024]{1,0:T(8,128)S(1)} %copy-done.31, f32[12,256,1024]{2,1,0:T(8,128)} %copy-done.1, f32[256,1024]{1,0:T(8,128)S(1)} %convolution_add_fusion.1, pred[256,1024]{1,0:T(8,128)(4,1)S(1)} %get-tuple-element.238), kind=kOutput, calls=%fused_computation.199 | output fusion | flops 22021120 | bytes 27537408 | tf_op jit(solution)/shard_map/sub | solution.py:169
  212.5 1.7 copy.74
  214.3 10.6 %fusion.128 = f32[12,64,256]{2,1,0:T(8,128)S(1)} fusion(bf16[1024,12,64]{0,2,1:T(8,128)(2,1)S(1)} %bitcast.266, f32[12,256,1024]{2,1,0:T(8,128)} %get-tuple-element.241, f32[12,256]{1,0:T(8,128)S(1)} %get-tuple-element.240), kind=kOutput, calls=%fused_computation.194 | convolution fusion | flops 2419064832 | bytes 14954496 | tf_op jit(solution)/shard_map/hqk,khd->qhd/dot_general | solution.py:172
  226.7 3.3 fusion.39
  230.1 3.8 fusion.31
  233.9 2.3 multiply_reduce_fusion
  236.3 2.4 copy.82
  238.7 1.5 fusion.131
  241.1 1.2 fusion.101
  242.3 1.5 convert_multiply_fusion
  243.8 1.2 copy.81
  245.0 11.4 %convolution_convert_fusion.1 = bf16[12,64,1024]{2,1,0:T(8,128)(2,1)} fusion(bf16[256,12,64]{0,2,1:T(8,128)(2,1)S(1)} %bitcast.277, f32[12,256,1024]{2,1,0:T(8,128)} %get-tuple-element.241, f32[12,256]{1,0:T(8,128)S(1)} %copy-done.64), kind=kOutput, calls=%fused_computation.60 | convolution fusion | flops 2419851264 | bytes 14561280 | tf_op jit(solution)/shard_map/hqk,qhd->khd/dot_general | solution.py:208
  256.8 11.6 %fusion.129 = (f32[1024]{0:T(1024)S(1)}, f32[256,1024]{1,0:T(8,128)}, f32[12,256,1024]{2,1,0:T(8,128)}) fusion(f32[12,256]{1,0:T(8,128)S(1)} %bitcast.284, bf16[256,12,64]{0,2,1:T(8,128)(2,1)} %bitcast.278, bf16[1024,12,64]{0,2,1:T(8,128)(2,1)} %bitcast.267, f32[12,256,1024]{2,1,0:T(8,128)} %get-tuple-element.241, f32[12,256]{1,0:T(8,128)S(1)} %copy-done.64), kind=kOutput, calls=%fused_computation.195 | convolution fusion | flops 418118656 | bytes 28209152 | tf_op jit(solution)/shard_map/qhd,khd->hqk/dot_general | solution.py:207
  268.4 8.0 %slice.78 = bf16[11,256,1024]{2,1,0:T(8,128)(2,1)} slice(f32[12,256,1024]{2,1,0:T(8,128)} %get-tuple-element.247), slice={[1:12], [0:256], [0:1024]} | slice | bytes 11534336 | tf_op jit(solution)/shard_map/slice | solution.py:220
  276.5 5.3 all-gather.1
  282.2 3.2 fusion.63
  285.5 5.2 multiply_convert_fusion
  291.7 0.9 copy.85
  292.6 3.0 convolution_bitcast_fusion
  295.6 5.8 copy.106
  301.4 9.1 %copy.86 = f32[6,128,24,128]{3,1,2,0:T(8,128)} copy(f32[6,128,24,128]{3,2,1,0:T(8,128)} %bitcast.238) | data formatting | bytes 18874368 | tf_op jit(solution)/shard_map/reshape | solution.py:49
  310.5 1.8 copy.101
  312.2 1.8 fusion.137
  314.0 5.6 fusion.62
  319.6 4.7 fusion.138
  324.3 4.0 fusion.93
  328.3 1.1 fusion.91
  329.5 1.9 copy.84
  331.4 1.3 pad_maximum_fusion.9
  332.7 2.1 fusion.136
  334.9 4.1 constant_dynamic-update-slice_fusion.3
  338.9 1.5 constant_dynamic-update-slice_fusion.2
  340.5 1.2 slice-done.3
  341.9 4.4 constant_dynamic-update-slice_fusion.1
  346.3 8.6 %constant_dynamic-update-slice_fusion = f32[433,128,128]{2,1,0:T(8,128)} fusion(f32[433,128,128]{2,1,0:T(8,128)} %constant_dynamic-update-slice_fusion.1, f32[144,128,128]{2,1,0:T(8,128)} %bitcast.237), kind=kLoop, calls=%fused_computation.152 | loop fusion | bytes 18874368
  355.5 26.1 %gather_fusion.1 = f32[448,128,128]{2,1,0:T(8,128)} fusion(f32[433,128,128]{2,1,0:T(8,128)} %broadcast_dynamic-update-slice_fusion, s32[1024]{0:T(1024)S(1)} %pad_clamp_fusion), kind=kCustom, calls=%fused_computation.1 | custom fusion | bytes 58722048 | tf_op jit(solution)/shard_map/gather | solution.py:77
  382.3 5.5 psum.14
  389.2 6.4 fusion.64
  395.6 57.1 %psum.15 = f32[2,768]{1,0:T(2,128)S(1)} all-reduce(f32[2,768]{1,0:T(2,128)S(1)} %pad_maximum_fusion.10), channel_id=1, replica_groups=mesh['dp'=8,'seq'=4] {'dp','seq'}, use_global_device_ids=true, to_apply=%region_26.27 | all-reduce | flops 1536 | bytes 12288 | tf_op jit(solution)/shard_map/psum | solution.py:254
  453.3 2.4 add_bitcast_fusion
  455.7 239.3 %reduce-scatter.8.cloned.1.call-done = f32[14,128,128]{2,1,0:T(8,128)} async-done(((f32[448,128,128]{2,1,0:T(8,128)}), f32[14,128,128]{2,1,0:T(8,128)}) %reduce-scatter.8.cloned.1.call-update) | async-done | bytes 917520 | tf_op jit(solution)/shard_map/reduce_scatter | solution.py:248
  695.1 3.1 fusion.139
  698.2 2.8 fusion.79
  701.0 1.5 fusion.80
  702.8 3.0 fusion.53
  (215 shorter events, 12.7 us)
Async XLA Ops:
  7.2 691.0 %copy-start = (f32[14,128,128]{2,1,0:T(8,128)S(1)}, f32[14,128,128]{2,1,0:T(8,128)}, u32[]{:S(2)}) copy-start(f32[14,128,128]{2,1,0:T(8,128)} %param.30) | copy-start | bytes 2752516
  7.2 112.1 %all-gather.6.cloned.1.call-start = ((), (), s32[]{:S(2)}) async-start(), calls=%async_computation.3 | async-start | bytes 15138816 | tf_op jit(solution)/shard_map/all_gather | solution.py:122
  9.4 167.3 %all-gather.10.cloned.1.call-start = ((), (), s32[]{:S(2)}) async-start(), calls=%async_computation.5 | async-start | bytes 1966080 | tf_op jit(solution)/shard_map/all_gather | solution.py:149
  12.2 129.8 %copy-start.42 = (f32[256]{0:T(256)}, f32[256]{0:T(256)S(1)}, u32[]{:S(2)}) copy-start(f32[256]{0:T(256)S(1)} %broadcast_multiply_fusion.2) | copy-start | bytes 3076
  14.0 128.0 %copy-start.44 = (f32[256]{0:T(256)}, f32[256]{0:T(256)S(1)}, u32[]{:S(2)}) copy-start(f32[256]{0:T(256)S(1)} %fusion.112) | copy-start | bytes 3076
  139.6 2.5 copy-start.8
  142.1 4.3 copy-start.39
  144.2 3.9 slice-start.1
  145.2 67.3 %all-gather.8.cloned.1.call-start = ((), (), s32[]{:S(2)}) async-start(), calls=%async_computation.4 | async-start | bytes 1966080 | tf_op jit(solution)/shard_map/all_gather | solution.py:150
  148.1 30.2 %copy-start.29 = (bf16[256,768]{0,1:T(8,128)(2,1)}, bf16[256,768]{0,1:T(8,128)(2,1)S(1)}, u32[]{:S(2)}) copy-start(bf16[256,768]{0,1:T(8,128)(2,1)S(1)} %copy.75) | copy-start | bytes 1179652
  176.6 147.7 %reduce-scatter.6.cloned.1.call-start = ((), (), s32[]{:S(2)}) async-start(), calls=%async_computation.7 | async-start | bytes 1966080 | tf_op jit(solution)/shard_map/reduce_scatter | solution.py:235
  178.4 6.6 copy-start.40
  178.4 6.5 copy-start.49
  178.4 6.5 copy-start.55
  178.4 6.5 copy-start.58
  180.3 4.7 copy-start.1
  186.2 8.4 %copy-start.31 = (f32[256,1024]{1,0:T(8,128)S(1)}, f32[256,1024]{1,0:T(8,128)}, u32[]{:S(2)}) copy-start(f32[256,1024]{1,0:T(8,128)} %get-tuple-element.239) | copy-start | bytes 3145732
  212.5 12.4 %copy-start.63 = (f32[12,256]{1,0:T(8,128)}, f32[12,256]{1,0:T(8,128)S(1)}, u32[]{:S(2)}) copy-start(f32[12,256]{1,0:T(8,128)S(1)} %get-tuple-element.240) | copy-start | bytes 36868
  214.2 10.7 %copy-start.27 = (bf16[1024,768]{0,1:T(8,128)(2,1)}, bf16[1024,768]{0,1:T(8,128)(2,1)S(1)}, u32[]{:S(2)}) copy-start(bf16[1024,768]{0,1:T(8,128)(2,1)S(1)} %copy.74) | copy-start | bytes 4718596
  214.2 12.4 %slice-start.7 = ((s8[4718592]{0:T(1024)(128)(4,1)}), s8[4194304]{0:T(1024)(128)(4,1)S(1)}, s32[]{:S(2)}) async-start(s8[4718592]{0:T(1024)(128)(4,1)} %bitcast.252), calls=%async_computation.16 | async-start | bytes 8388608
  214.3 11.6 %copy-start.12 = (bf16[6,6,128,128]{3,1,2,0:T(8,128)(2,1)S(1)}, bf16[6,6,128,128]{3,1,2,0:T(8,128)(2,1)}, u32[]{:S(2)}) copy-start(bf16[6,6,128,128]{3,1,2,0:T(8,128)(2,1)} %copy.77) | copy-start | bytes 3538948
  214.3 12.4 %slice-start.8 = ((s8[4718592]{0:T(1024)(128)(4,1)}), s8[524288]{0:T(1024)(128)(4,1)S(1)}, s32[]{:S(2)}) async-start(s8[4718592]{0:T(1024)(128)(4,1)} %bitcast.252), calls=%async_computation.17 | async-start | bytes 1048576
  225.0 5.1 copy-start.23
  225.8 4.2 slice-start.5
  226.4 66.2 %copy-start.4 = (f32[256,768]{1,0:T(8,128)}, f32[256,768]{1,0:T(8,128)S(1)}, u32[]{:S(2)}) copy-start(f32[256,768]{1,0:T(8,128)S(1)} %get-tuple-element.243) | copy-start | bytes 2359300
  226.7 3.4 slice-start.6
  226.7 3.4 copy-start.18
  230.1 3.9 copy-start.62
  236.3 6.0 copy-start.13
  238.7 3.6 copy-start.22
  240.2 4.8 copy-start.64
  245.0 11.4 %copy-start.35 = (bf16[256,768]{0,1:T(8,128)(2,1)}, bf16[256,768]{0,1:T(8,128)(2,1)S(1)}, u32[]{:S(2)}) copy-start(bf16[256,768]{0,1:T(8,128)(2,1)S(1)} %copy.81) | copy-start | bytes 1179652
  245.0 11.5 %copy-start.21 = (f32[256,768]{1,0:T(8,128)S(1)}, f32[256,768]{1,0:T(8,128)}, u32[]{:S(2)}) copy-start(f32[256,768]{1,0:T(8,128)} %get-tuple-element.245) | copy-start | bytes 2359300
  256.4 67.8 %reduce-scatter.4.cloned.1.call-start = ((), (), s32[]{:S(2)}) async-start(), calls=%async_computation.6 | async-start | bytes 1966080 | tf_op jit(solution)/shard_map/reduce_scatter | solution.py:229
  268.4 13.8 %copy-start.41 = (s32[1,1024]{1,0:T(1,128)S(1)}, s32[1,1024]{1,0:T(1,128)}, u32[]{:S(2)}) copy-start(s32[1,1024]{1,0:T(1,128)} %param.19) | copy-start | bytes 12292
  268.4 13.8 %copy-start.50 = (s32[1,256]{1,0:T(1,128)S(1)}, s32[1,256]{1,0:T(1,128)}, u32[]{:S(2)}) copy-start(s32[1,256]{1,0:T(1,128)} %copy-done.48) | copy-start | bytes 3076
  268.4 13.8 %copy-start.56 = (s32[256]{0:T(256)S(1)}, s32[256]{0:T(256)}, u32[]{:S(2)}) copy-start(s32[256]{0:T(256)} %copy-done.54) | copy-start | bytes 3076
  268.4 13.8 %copy-start.59 = (pred[1024]{0:T(1024)(128)(4,1)S(1)}, pred[1024]{0:T(1024)(128)(4,1)}, u32[]{:S(2)}) copy-start(pred[1024]{0:T(1024)(128)(4,1)} %copy-done.57) | copy-start | bytes 3076
  276.5 9.0 %copy-start.30 = (bf16[256,768]{0,1:T(8,128)(2,1)S(1)}, bf16[256,768]{0,1:T(8,128)(2,1)}, u32[]{:S(2)}) copy-start(bf16[256,768]{0,1:T(8,128)(2,1)} %copy-done.29) | copy-start | bytes 1179652
  285.5 5.2 copy-start.60
  285.5 5.3 copy-start.19
  285.5 6.2 copy-start.51
  285.5 6.2 copy-start.17
  290.7 404.4 %reduce-scatter.8.cloned.1.call-start = ((), (), s32[]{:S(2)}) async-start(), calls=%async_computation.8 | async-start | bytes 30277632 | tf_op jit(solution)/shard_map/reduce_scatter | solution.py:248
  301.4 9.1 %copy-start.26 = (bf16[3072,256]{0,1:T(8,128)(2,1)S(1)}, bf16[3072,256]{0,1:T(8,128)(2,1)}, u32[]{:S(2)}) copy-start(bf16[3072,256]{0,1:T(8,128)(2,1)} %get-tuple-element.250) | copy-start | bytes 4718596
  314.0 5.6 copy-start.11
  314.0 5.6 copy-start.25
  319.6 4.7 copy-start.43
  324.3 4.0 copy-start.47
  324.3 4.1 copy-start.9
  324.3 4.1 copy-start.45
  334.8 5.7 slice-start.2
  334.8 6.9 slice-start.3
  334.9 7.1 slice-start.4
  381.5 7.5 %copy-start.5 = (f32[256,768]{1,0:T(8,128)S(1)}, f32[256,768]{1,0:T(8,128)}, u32[]{:S(2)}) copy-start(f32[256,768]{1,0:T(8,128)} %copy-done.4) | copy-start | bytes 2359300
  389.1 63.6 %copy-start.38 = (f32[2,768]{1,0:T(2,128)S(1)}, f32[2,768]{1,0:T(2,128)}, u32[]{:S(2)}) copy-start(f32[2,768]{1,0:T(2,128)} %param.22) | copy-start | bytes 18436
  389.1 63.6 %copy-start.52 = (f32[2,768]{1,0:T(2,128)S(1)}, f32[2,768]{1,0:T(2,128)}, u32[]{:S(2)}) copy-start(f32[2,768]{1,0:T(2,128)} %param.23) | copy-start | bytes 18436
  389.1 63.6 %copy-start.53 = (f32[2,768]{1,0:T(2,128)S(1)}, f32[2,768]{1,0:T(2,128)}, u32[]{:S(2)}) copy-start(f32[2,768]{1,0:T(2,128)} %param.24) | copy-start | bytes 18436
  389.1 64.2 %copy-start.3 = (f32[256,768]{1,0:T(8,128)S(1)}, f32[256,768]{1,0:T(8,128)}, u32[]{:S(2)}) copy-start(f32[256,768]{1,0:T(8,128)} %copy-done.2) | copy-start | bytes 2359300
  389.1 64.2 %copy-start.10 = (bf16[1,256,768]{2,1,0:T(8,128)(2,1)S(1)}, bf16[1,256,768]{2,1,0:T(8,128)(2,1)}, u32[]{:S(2)}) copy-start(bf16[1,256,768]{2,1,0:T(8,128)(2,1)} %param.18) | copy-start | bytes 1179652
  389.1 64.2 %copy-start.20 = (bf16[1,256,768]{2,1,0:T(8,128)(2,1)S(1)}, bf16[1,256,768]{2,1,0:T(8,128)(2,1)}, u32[]{:S(2)}) copy-start(bf16[1,256,768]{2,1,0:T(8,128)(2,1)} %param.31) | copy-start | bytes 1179652
  698.2 2.8 copy-start.32
  701.0 4.8 copy-start.33
  701.0 4.8 copy-start.34
  (16 other events, 23.9 us)
Sparse Core Ops, SparseCore 0:
  11.4 107.8 all-gather.5
  145.3 17.7 all-gather.9
  176.7 18.1 all-gather.7
  256.6 26.2 reduce-scatter.5
  290.8 25.6 reduce-scatter.3
  381.7 313.3 reduce-scatter.7
where the time goes:
time: 721 us; the launch traced here: 714 us
  waiting for transfers between devices  345 us (48%)
  local copies, waits for them, and re-layouts  144 us (20%)
  matrix products  97 us (13%)
  blocking collectives  73.4 us (10%)
  other arithmetic  35.5 us (5%)
  between operations  18.5 us (3%)
    reduce_scatter x1, waiting for transfers between devices, local(): lax.psum_scatter(slot_buffer(grad_sums, slot_tiles, tile_side, tile_count...  239 us
    all_gather x1, waiting for transfers between devices, local(): lax.all_gather(weight_slots.astype(jnp.bfloat16), ('dp', 'seq'), axis=0,...  105 us
    psum x1, blocking collectives, local(): gain_total = lax.psum(gain_grad, ('dp', 'seq'))  57.1 us
    unnamed x149, local copies, waits for them, and re-layouts  34 us
    gather x1, local copies, waits for them, and re-layouts, slot_buffer(): return stacked[jnp.minimum(slot_tiles, tile_count)]  26.1 us
    reshape x4, local copies, waits for them, and re-layouts, matrix_of(): tile_stack.reshape(height // tile_side, across // tile_side, tile_side, t...  18.8 us
    gather x1, local copies, waits for them, and re-layouts, local(): shared[position]  18.3 us
    sub x1, other arithmetic, local(): exps = jnp.exp(logits - row_max[:, :, None]) * allowed_float[None]  17.9 us
  transfers between devices with their start and end apart: 6, of which 2 were waited for; matrix products, arithmetic and copies ran while one was open for 18% of the time, Pallas kernels for 0%

commit v1 on v0

--- a/solution.py
+++ b/solution.py
@@ -17,6 +17,28 @@
 decay_rate = 0.1
 norm_epsilon = 1e-05
 precise = lax.Precision.HIGHEST
+
+
+def laid_out(pieces, dim):
+    shape = list(pieces.shape[1:])
+    shape[dim] *= pieces.shape[0]
+    return jnp.moveaxis(pieces, 0, dim).reshape(shape)
+
+
+def doubled(x, axis):
+    size = lax.axis_size(axis)
+    blocks = x[None]
+    for level in range(size.bit_length() - 1):
+        stride = 1 << level
+        partner_block = lax.ppermute(blocks, axis, [(i, i ^ stride) for i in range(size)])
+        both = jnp.stack([blocks, partner_block])
+        upper = lax.axis_index(axis) >> level & 1
+        blocks = jnp.where(upper == 0, both, both[::-1]).reshape(-1, *x.shape)
+    return blocks
+
+
+def doubled_up(value, axis, dim):
+    return laid_out(doubled(value, axis), dim)
 
 
 def carried_in(value, axis, join, neutral, backward):
@@ -119,7 +141,7 @@
     query_start = lax.axis_index("seq") * tok_local
     query_pos = query_start + jnp.arange(tok_local, dtype=jnp.int32)
     key_pos = jnp.arange(length, dtype=jnp.int32)
-    shared = lax.all_gather(weight_slots.astype(jnp.bfloat16), ("dp", "seq"), axis=0, tiled=True)
+    shared = doubled_up(weight_slots.astype(jnp.bfloat16), ("dp", "seq"), 0)
     tile_ids = jnp.arange(tile_count, dtype=jnp.int32)
     slot_ids = jnp.arange(slot_total, dtype=jnp.int32)
     position = jnp.sum(

time: 721 us -> 1110 us (1.54)
  waiting for transfers between devices: 345 us -> 707 us
  other arithmetic: 35.5 us -> 64.7 us
    ppermute x0 -> x5, waiting for transfers between devices: none -> 456 us  [doubled(): lax.ppermute(blocks, axis, [(i, i ^ stride) for i in range(size)])]
    all_gather x1 -> x0, waiting for transfers between devices: 105 us -> none  [local(): lax.all_gather(weight_slots.astype(jnp.bfloat16), ('dp', 'seq'), axis=0,...]
    transpose x0 -> x4, local copies, waits for them, and re-layouts: none -> 19.4 us  [matrix_of(): return shaped.transpose(0, 2, 1, 3).reshape(height, across)]
    reshape x4 -> x0, local copies, waits for them, and re-layouts: 18.8 us -> none  [matrix_of(): tile_stack.reshape(height // tile_side, across // tile_side, tile_side, t...]
    select_n x0 -> x4, other arithmetic: none -> 17 us  [doubled(): blocks = jnp.where(upper == 0, both, both[::-1]).reshape(-1, *x.shape)]
    another operation x0 -> x7, other arithmetic: none -> 16.4 us  [doubled(): both = jnp.stack([blocks, partner_block])]
    reduce_scatter x1, waiting for transfers between devices: 239 us -> 251 us  [local(): lax.psum_scatter(slot_buffer(grad_sums, slot_tiles, tile_side, tile_count...]
  transfers between devices with their start and end apart: 6 -> 10, of which waited for: 2 -> 6; matrix products, arithmetic and copies ran while one was open for 18% -> 12% of each run, Pallas kernels for 0% -> 0%
where the time goes in v1:
time: 1110 us; the launch traced here: 1100 us
  waiting for transfers between devices  707 us (64%)
  local copies, waits for them, and re-layouts  143 us (13%)
  matrix products  97 us (9%)
  other arithmetic  64.7 us (6%)
  blocking collectives  64.5 us (6%)
  between operations  18.3 us (2%)
    ppermute x5, waiting for transfers between devices, doubled(): lax.ppermute(blocks, axis, [(i, i ^ stride) for i in range(size)])  456 us
    reduce_scatter x1, waiting for transfers between devices, local(): lax.psum_scatter(slot_buffer(grad_sums, slot_tiles, tile_side, tile_count...  251 us
    psum x1, blocking collectives, local(): gain_total = lax.psum(gain_grad, ('dp', 'seq'))  47.8 us
    unnamed x149, local copies, waits for them, and re-layouts  33.1 us
    gather x1, local copies, waits for them, and re-layouts, slot_buffer(): return stacked[jnp.minimum(slot_tiles, tile_count)]  26.1 us
  transfers between devices with their start and end apart: 10, of which 6 were waited for; matrix products, arithmetic and copies ran while one was open for 12% of the time, Pallas kernels for 0%

profile of v1, /device:TPU:1, one launch (start us, length us, event | category | flops | bytes accessed | tf_op | source)
XLA Modules:
  0.0 1100.7 jit_solution(9216307372026073719)
XLA Ops:
  8.8 1.8 collective-permute-done
  12.0 2.4 collective-permute-start.1
  14.4 20.6 %collective-permute-done.1 = bf16[2,14,128,128]{3,2,1,0:T(8,128)(2,1)S(1)} collective-permute-done((bf16[2,14,128,128]{3,2,1,0:T(8,128)(2,1)}, bf16[2,14,128,128]{3,2,1,0:T(8,128)(2,1)S(1)}, u32[]{:S(2)}, u32[]{:S(2)}) %collective-permute-start.1) | collective-permute-done | bytes 917536 | tf_op jit(solution)/shard_map/ppermute | solution.py:33
  36.9 39.6 %collective-permute-done.2 = bf16[4,14,128,128]{3,2,1,0:T(8,128)(2,1)} collective-permute-done((bf16[4,14,128,128]{3,2,1,0:T(8,128)(2,1)S(1)}, bf16[4,14,128,128]{3,2,1,0:T(8,128)(2,1)}, u32[]{:S(2)}, u32[]{:S(2)}) %collective-permute-start.2) | collective-permute-done | bytes 1835040 | tf_op jit(solution)/shard_map/ppermute | solution.py:33
  76.5 1.8 pad_maximum_fusion.5
  78.4 2.8 reverse_select_fusion.2
  82.1 78.5 %collective-permute-done.3 = bf16[8,14,128,128]{3,2,1,0:T(8,128)(2,1)} collective-permute-done((bf16[8,14,128,128]{3,2,1,0:T(8,128)(2,1)}, bf16[8,14,128,128]{3,2,1,0:T(8,128)(2,1)}, u32[]{:S(2)}, u32[]{:S(2)}) %collective-permute-start.3) | collective-permute-done | bytes 3670048 | tf_op jit(solution)/shard_map/ppermute | solution.py:33
  160.6 3.8 pad_maximum_fusion.1
  164.4 6.2 reverse_select_fusion.1
  170.7 1.5 collective-permute-start.4
  173.5 315.4 %collective-permute-done.4 = bf16[16,14,128,128]{3,2,1,0:T(8,128)(2,1)} collective-permute-done((bf16[16,14,128,128]{3,2,1,0:T(8,128)(2,1)}, bf16[16,14,128,128]{3,2,1,0:T(8,128)(2,1)}, u32[]{:S(2)}, u32[]{:S(2)}) %collective-permute-start.4) | collective-permute-done | bytes 7340064 | tf_op jit(solution)/shard_map/ppermute | solution.py:33
  488.8 7.6 pad_maximum_fusion
  496.5 7.4 reverse_select_fusion
  503.9 18.3 %gather_fusion = bf16[432,128,128]{2,1,0:T(8,128)(2,1)} fusion(bf16[448,128,128]{2,1,0:T(8,128)(2,1)} %bitcast.256, s32[1024]{0:T(1024)S(1)} %get-tuple-element.257), kind=kCustom, calls=%fused_computation | custom fusion | bytes 28313280 | tf_op jit(solution)/shard_map/gather | solution.py:150
  522.2 2.0 slice-done
  524.2 2.4 copy.89
  530.6 1.5 fusion.71
  532.3 2.0 copy.93
  534.2 11.9 %fusion.134 = (bf16[144,128,128]{2,1,0:T(8,128)(2,1)}, bf16[144,128,128]{2,1,0:T(8,128)(2,1)}) fusion(bf16[432,128,128]{2,1,0:T(8,128)(2,1)} %gather_fusion), kind=kLoop, calls=%fused_computation.211 | loop fusion | bytes 18874368 | tf_op jit(solution)/shard_map/slice | solution.py:88
  546.2 7.4 copy.95
  553.6 7.5 copy.94
  561.2 1.7 copy.92
  563.0 1.8 broadcast_multiply_fusion
  564.8 4.6 copy-done.1
  570.7 6.0 all-gather
  577.1 2.6 convolution_add_fusion.1
  579.8 18.0 %fusion.136 = (f32[12,256]{1,0:T(8,128)S(1)}, f32[12,256,1024]{2,1,0:T(8,128)}) fusion(f32[256,1024]{1,0:T(8,128)S(1)} %copy-done.30, f32[12,256,1024]{2,1,0:T(8,128)} %copy-done.1, f32[256,1024]{1,0:T(8,128)S(1)} %convolution_add_fusion.1, pred[256,1024]{1,0:T(8,128)(4,1)S(1)} %get-tuple-element.242), kind=kOutput, calls=%fused_computation.213 | output fusion | flops 22021120 | bytes 27537408 | tf_op jit(solution)/shard_map/sub | solution.py:191
  597.8 1.7 copy.90
  599.5 10.6 fusion.130
  612.0 3.3 fusion.39
  615.3 3.8 fusion.31
  619.2 2.3 multiply_reduce_fusion
  621.5 2.4 copy.98
  623.9 1.5 fusion.133
  627.5 1.5 convert_multiply_fusion
  630.3 11.4 %convolution_convert_fusion.1 = bf16[12,64,1024]{2,1,0:T(8,128)(2,1)} fusion(bf16[256,12,64]{0,2,1:T(8,128)(2,1)S(1)} %bitcast.306, f32[12,256,1024]{2,1,0:T(8,128)} %get-tuple-element.245, f32[12,256]{1,0:T(8,128)S(1)} %copy-done.64), kind=kOutput, calls=%fused_computation.68 | convolution fusion | flops 2419851264 | bytes 14561280 | tf_op jit(solution)/shard_map/hqk,qhd->khd/dot_general | solution.py:230
  642.1 11.3 %fusion.131 = (f32[1024]{0:T(1024)S(1)}, f32[256,1024]{1,0:T(8,128)}, f32[12,256,1024]{2,1,0:T(8,128)}) fusion(f32[12,256]{1,0:T(8,128)S(1)} %bitcast.313, bf16[256,12,64]{0,2,1:T(8,128)(2,1)} %bitcast.307, bf16[1024,12,64]{0,2,1:T(8,128)(2,1)} %bitcast.294, f32[12,256,1024]{2,1,0:T(8,128)} %get-tuple-element.245, f32[12,256]{1,0:T(8,128)S(1)} %copy-done.64), kind=kOutput, calls=%fused_computation.209 | convolution fusion | flops 418118656 | bytes 28209152 | tf_op jit(solution)/shard_map/qhd,khd->hqk/dot_general | solution.py:229
  653.4 7.8 slice.78
  661.2 5.3 all-gather.1
  667.0 3.2 fusion.63
  670.3 5.2 multiply_convert_fusion
  677.4 2.9 convolution_bitcast_fusion
  680.3 5.8 copy.122
  686.1 9.1 copy.102
  695.2 1.7 copy.117
  697.0 1.6 fusion.139
  698.6 6.1 fusion.62
  704.7 4.7 fusion.140
  709.5 4.0 fusion.93
  714.7 1.9 copy.100
  717.9 2.1 fusion.138
  720.1 4.1 constant_dynamic-update-slice_fusion.3
  724.2 1.5 constant_dynamic-update-slice_fusion.2
  727.1 4.4 constant_dynamic-update-slice_fusion.1
  731.5 8.6 constant_dynamic-update-slice_fusion
  740.7 26.1 %gather_fusion.1 = f32[448,128,128]{2,1,0:T(8,128)} fusion(f32[433,128,128]{2,1,0:T(8,128)} %broadcast_dynamic-update-slice_fusion, s32[1024]{0:T(1024)S(1)} %copy-done.46), kind=kCustom, calls=%fused_computation.1 | custom fusion | bytes 58722048 | tf_op jit(solution)/shard_map/gather | solution.py:99
  767.6 5.4 psum.14
  774.4 6.3 fusion.64
  780.6 47.8 %psum.15 = f32[2,768]{1,0:T(2,128)S(1)} all-reduce(f32[2,768]{1,0:T(2,128)S(1)} %pad_maximum_fusion.15), channel_id=1, replica_groups=mesh['dp'=8,'seq'=4] {'dp','seq'}, use_global_device_ids=true, to_apply=%region_26.27 | all-reduce | flops 1536 | bytes 12288 | tf_op jit(solution)/shard_map/psum | solution.py:276
  829.1 2.4 add_bitcast_fusion
  831.5 250.9 %reduce-scatter.8.cloned.1.call-done = f32[14,128,128]{2,1,0:T(8,128)} async-done(((f32[448,128,128]{2,1,0:T(8,128)}), f32[14,128,128]{2,1,0:T(8,128)}) %reduce-scatter.8.cloned.1.call-update) | async-done | bytes 917520 | tf_op jit(solution)/shard_map/reduce_scatter | solution.py:270
  1082.4 3.1 fusion.141
  1085.5 2.8 fusion.79
  1089.8 3.0 fusion.53
  (231 shorter events, 27.2 us)
Async XLA Ops:
  7.2 1078.3 %copy-start = (f32[14,128,128]{2,1,0:T(8,128)S(1)}, f32[14,128,128]{2,1,0:T(8,128)}, u32[]{:S(2)}) copy-start(f32[14,128,128]{2,1,0:T(8,128)} %param.30) | copy-start | bytes 2752516
  7.2 554.0 %all-gather.7.cloned.1.call-start = ((), (), s32[]{:S(2)}) async-start(), calls=%async_computation.4 | async-start | bytes 1966080 | tf_op jit(solution)/shard_map/all_gather | solution.py:171
  8.7 1.9 collective-permute-start
  12.0 23.0 %collective-permute-start.1 = (bf16[2,14,128,128]{3,2,1,0:T(8,128)(2,1)}, bf16[2,14,128,128]{3,2,1,0:T(8,128)(2,1)S(1)}, u32[]{:S(2)}, u32[]{:S(2)}) collective-permute-start(bf16[2,14,128,128]{3,2,1,0:T(8,128)(2,1)} %get-tuple-element.236), channel_id=1, source_target_pairs={{0,2},{1,3},{2,0},{3,1},{4,6},{5,7},{6,4},{7,5},{8,10},{9,11},{10,... | collective-permute-start | bytes 2752520 | tf_op jit(solution)/shard_map/ppermute | solution.py:33
  35.7 40.8 %collective-permute-start.2 = (bf16[4,14,128,128]{3,2,1,0:T(8,128)(2,1)S(1)}, bf16[4,14,128,128]{3,2,1,0:T(8,128)(2,1)}, u32[]{:S(2)}, u32[]{:S(2)}) collective-permute-start(bf16[4,14,128,128]{3,2,1,0:T(8,128)(2,1)S(1)} %bitcast.268), channel_id=1, source_target_pairs={{0,4},{1,5},{2,6},{3,7},{4,0},{5,1},{6,2},{7,3},{8,12},{9,13},{10,... | collective-permute-start | bytes 5505032 | tf_op jit(solution)/shard_map/ppermute | solution.py:33
  81.2 79.4 %collective-permute-start.3 = (bf16[8,14,128,128]{3,2,1,0:T(8,128)(2,1)}, bf16[8,14,128,128]{3,2,1,0:T(8,128)(2,1)}, u32[]{:S(2)}, u32[]{:S(2)}) collective-permute-start(bf16[8,14,128,128]{3,2,1,0:T(8,128)(2,1)} %bitcast.12), channel_id=1, source_target_pairs={{0,8},{1,9},{2,10},{3,11},{4,12},{5,13},{6,14},{7,15},{8,0},{9,1},... | collective-permute-start | bytes 11010056 | tf_op jit(solution)/shard_map/ppermute | solution.py:33
  164.4 7.8 copy-start.52
  164.4 8.6 copy-start.37
  164.4 8.6 copy-start.7
  170.7 318.2 %collective-permute-start.4 = (bf16[16,14,128,128]{3,2,1,0:T(8,128)(2,1)}, bf16[16,14,128,128]{3,2,1,0:T(8,128)(2,1)}, u32[]{:S(2)}, u32[]{:S(2)}) collective-permute-start(bf16[16,14,128,128]{3,2,1,0:T(8,128)(2,1)} %bitcast.15), channel_id=1, source_target_pairs={{0,16},{1,17},{2,18},{3,19},{4,20},{5,21},{6,22},{7,23},{8,24},{9,... | collective-permute-start | bytes 22020104 | tf_op jit(solution)/shard_map/ppermute | solution.py:33
  173.2 353.5 %copy-start.42 = (f32[256]{0:T(256)}, f32[256]{0:T(256)S(1)}, u32[]{:S(2)}) copy-start(f32[256]{0:T(256)S(1)} %broadcast_multiply_fusion.2) | copy-start | bytes 3076
  173.4 323.0 %copy-start.47 = (f32[256]{0:T(256)}, f32[256]{0:T(256)S(1)}, u32[]{:S(2)}) copy-start(f32[256]{0:T(256)S(1)} %fusion.92) | copy-start | bytes 3076
  173.5 353.2 %copy-start.44 = (f32[256]{0:T(256)}, f32[256]{0:T(256)S(1)}, u32[]{:S(2)}) copy-start(f32[256]{0:T(256)S(1)} %fusion.114) | copy-start | bytes 3076
  529.8 68.0 %all-gather.5.cloned.1.call-start = ((), (), s32[]{:S(2)}) async-start(), calls=%async_computation.3 | async-start | bytes 1966080 | tf_op jit(solution)/shard_map/all_gather | solution.py:172
  532.2 30.7 %copy-start.28 = (bf16[256,768]{0,1:T(8,128)(2,1)}, bf16[256,768]{0,1:T(8,128)(2,1)S(1)}, u32[]{:S(2)}) copy-start(bf16[256,768]{0,1:T(8,128)(2,1)S(1)} %copy.91) | copy-start | bytes 1179652
  561.1 148.3 %reduce-scatter.6.cloned.1.call-start = ((), (), s32[]{:S(2)}) async-start(), calls=%async_computation.6 | async-start | bytes 1966080 | tf_op jit(solution)/shard_map/reduce_scatter | solution.py:257
  563.0 6.5 copy-start.40
  563.0 6.5 copy-start.50
  563.0 6.4 copy-start.56
  563.0 6.4 copy-start.59
  564.8 4.6 copy-start.1
  570.7 9.0 copy-start.30
  597.8 12.4 %copy-start.63 = (f32[12,256]{1,0:T(8,128)}, f32[12,256]{1,0:T(8,128)S(1)}, u32[]{:S(2)}) copy-start(f32[12,256]{1,0:T(8,128)S(1)} %get-tuple-element.244) | copy-start | bytes 36868
  599.5 10.7 copy-start.26
  599.5 12.4 %slice-start.7 = ((s8[4718592]{0:T(1024)(128)(4,1)}), s8[4194304]{0:T(1024)(128)(4,1)S(1)}, s32[]{:S(2)}) async-start(s8[4718592]{0:T(1024)(128)(4,1)} %bitcast.279), calls=%async_computation.15 | async-start | bytes 8388608
  599.5 11.6 %copy-start.11 = (bf16[6,128,6,128]{3,2,1,0:T(8,128)(2,1)S(1)}, bf16[6,128,6,128]{3,2,1,0:T(8,128)(2,1)}, u32[]{:S(2)}) copy-start(bf16[6,128,6,128]{3,2,1,0:T(8,128)(2,1)} %copy.93) | copy-start | bytes 3538948
  599.5 12.4 %slice-start.8 = ((s8[4718592]{0:T(1024)(128)(4,1)}), s8[524288]{0:T(1024)(128)(4,1)S(1)}, s32[]{:S(2)}) async-start(s8[4718592]{0:T(1024)(128)(4,1)} %bitcast.279), calls=%async_computation.16 | async-start | bytes 1048576
  610.2 5.1 copy-start.22
  611.1 4.2 slice-start.5
  611.7 65.7 %copy-start.4 = (f32[256,768]{1,0:T(8,128)}, f32[256,768]{1,0:T(8,128)S(1)}, u32[]{:S(2)}) copy-start(f32[256,768]{1,0:T(8,128)S(1)} %get-tuple-element.247) | copy-start | bytes 2359300
  621.5 6.0 copy-start.12
  625.5 4.8 copy-start.64
  630.3 11.4 %copy-start.34 = (bf16[256,768]{0,1:T(8,128)(2,1)}, bf16[256,768]{0,1:T(8,128)(2,1)S(1)}, u32[]{:S(2)}) copy-start(bf16[256,768]{0,1:T(8,128)(2,1)S(1)} %copy.97) | copy-start | bytes 1179652
  630.3 11.5 %copy-start.20 = (f32[256,768]{1,0:T(8,128)S(1)}, f32[256,768]{1,0:T(8,128)}, u32[]{:S(2)}) copy-start(f32[256,768]{1,0:T(8,128)} %get-tuple-element.249) | copy-start | bytes 2359300
  641.7 67.8 %reduce-scatter.4.cloned.1.call-start = ((), (), s32[]{:S(2)}) async-start(), calls=%async_computation.5 | async-start | bytes 1966080 | tf_op jit(solution)/shard_map/reduce_scatter | solution.py:251
  653.4 13.5 %copy-start.41 = (s32[1,1024]{1,0:T(1,128)S(1)}, s32[1,1024]{1,0:T(1,128)}, u32[]{:S(2)}) copy-start(s32[1,1024]{1,0:T(1,128)} %param.19) | copy-start | bytes 12292
  653.4 13.5 %copy-start.51 = (s32[1,256]{1,0:T(1,128)S(1)}, s32[1,256]{1,0:T(1,128)}, u32[]{:S(2)}) copy-start(s32[1,256]{1,0:T(1,128)} %copy-done.49) | copy-start | bytes 3076
  653.4 13.5 %copy-start.57 = (s32[256]{0:T(256)S(1)}, s32[256]{0:T(256)}, u32[]{:S(2)}) copy-start(s32[256]{0:T(256)} %copy-done.55) | copy-start | bytes 3076
  653.4 13.5 %copy-start.60 = (pred[1024]{0:T(1024)(128)(4,1)S(1)}, pred[1024]{0:T(1024)(128)(4,1)}, u32[]{:S(2)}) copy-start(pred[1024]{0:T(1024)(128)(4,1)} %copy-done.58) | copy-start | bytes 3076
  661.2 9.0 copy-start.29
  670.2 5.2 copy-start.61
  670.2 5.3 copy-start.18
  670.2 6.2 copy-start.16
  675.4 407.0 %reduce-scatter.8.cloned.1.call-start = ((), (), s32[]{:S(2)}) async-start(), calls=%async_computation.7 | async-start | bytes 30277632 | tf_op jit(solution)/shard_map/reduce_scatter | solution.py:270
  686.1 9.1 copy-start.25
  698.6 6.1 copy-start.10
  698.6 6.1 copy-start.24
  704.7 4.7 copy-start.43
  709.5 4.1 copy-start.8
  720.0 5.6 slice-start.2
  720.1 6.9 slice-start.3
  720.1 7.1 slice-start.4
  731.5 9.2 copy-start.46
  766.8 7.5 copy-start.5
  774.3 54.1 %copy-start.38 = (f32[2,768]{1,0:T(2,128)S(1)}, f32[2,768]{1,0:T(2,128)}, u32[]{:S(2)}) copy-start(f32[2,768]{1,0:T(2,128)} %param.22) | copy-start | bytes 18436
  774.3 54.1 %copy-start.53 = (f32[2,768]{1,0:T(2,128)S(1)}, f32[2,768]{1,0:T(2,128)}, u32[]{:S(2)}) copy-start(f32[2,768]{1,0:T(2,128)} %param.23) | copy-start | bytes 18436
  774.3 54.1 %copy-start.54 = (f32[2,768]{1,0:T(2,128)S(1)}, f32[2,768]{1,0:T(2,128)}, u32[]{:S(2)}) copy-start(f32[2,768]{1,0:T(2,128)} %param.24) | copy-start | bytes 18436
  774.3 54.8 %copy-start.3 = (f32[256,768]{1,0:T(8,128)S(1)}, f32[256,768]{1,0:T(8,128)}, u32[]{:S(2)}) copy-start(f32[256,768]{1,0:T(8,128)} %copy-done.2) | copy-start | bytes 2359300
  774.3 54.7 %copy-start.9 = (bf16[1,256,768]{2,1,0:T(8,128)(2,1)S(1)}, bf16[1,256,768]{2,1,0:T(8,128)(2,1)}, u32[]{:S(2)}) copy-start(bf16[1,256,768]{2,1,0:T(8,128)(2,1)} %param.18) | copy-start | bytes 1179652
  774.4 54.7 %copy-start.19 = (bf16[1,256,768]{2,1,0:T(8,128)(2,1)S(1)}, bf16[1,256,768]{2,1,0:T(8,128)(2,1)}, u32[]{:S(2)}) copy-start(bf16[1,256,768]{2,1,0:T(8,128)(2,1)} %param.31) | copy-start | bytes 1179652
  831.5 256.8 %copy-start.31 = (f32[14,128,128]{2,1,0:T(8,128)S(1)}, f32[14,128,128]{2,1,0:T(8,128)}, u32[]{:S(2)}) copy-start(f32[14,128,128]{2,1,0:T(8,128)} %param.29) | copy-start | bytes 2752516
  1085.5 4.3 copy-start.14
  1088.3 4.5 copy-start.32
  1088.3 4.5 copy-start.33
  (20 other events, 47.6 us)
Sparse Core Ops, SparseCore 0:
  529.9 20.4 all-gather.6
  561.3 20.4 all-gather.4
  641.8 27.8 reduce-scatter.5
  675.6 27.7 reduce-scatter.3
  767.0 315.4 reduce-scatter.7
